TPU v7x, 32 devices: a whole 2x2x4 slice. The times are simulated.
32 devices in a mesh: row: 4 (over z), leaf: 8 (over y, x, core).
Axes of the slice: x: 2, y: 2, z: 4, core: 2. Of those that a mesh axis runs over, the one named last changes fastest.
Arguments:
- leaf_update: float32 [16384, 256], P(('leaf', 'row')), may hold values from -6 to 6
- rhs: float32 [3, 16384, 256], P(None, ('leaf', 'row')), may hold values from -6 to 6
- inv_top: bfloat16 [2, 16384, 8, 4, 512], P(None, 'leaf', None, 'row'), may hold values from -0.03125 to 0.03125
- inv_mid: bfloat16 [2, 16384, 4, 4, 512], P(None, 'leaf', None, 'row'), may hold values from -0.046875 to 0.046875
- inv_low: bfloat16 [2, 16384, 2, 4, 512], P(None, 'leaf', None, 'row'), may hold values from -0.0625 to 0.0625
- couple_mid: bfloat16 [2, 16384, 4, 4, 512], P(None, 'leaf', None, 'row'), may hold values from -0.046875 to 0.046875
- couple_low: bfloat16 [2, 16384, 2, 4, 512], P(None, 'leaf', None, 'row'), may hold values from -0.0625 to 0.0625
- block_map: int32 [3, 128], P(None, ('leaf', 'row')), may hold values from 0 to 127, as said below
Outputs:
- solution: float32 [3, 16384, 256], P(None, ('leaf', 'row'))
- leaf_solution: float32 [16384, 256], P(('leaf', 'row'))
Inputs may be any that keep to these rules, and one draw needn't show every extreme that they name: Device d of the group of a front holds rows d * 512 to (d + 1) * 512 - 1 of the front's separator part and the same rows of its update part, with d = p * 4 + r for group position p (leaf index modulo the group size) and row index r. block_map[k] is one to one within each parent, and a block held at row index r and group position p of a child lands on a parent block held at row index r and group position p or p + (group size of the parent) / 2. At level 0 every parent block receives one block.
All inputs are finite; a program needn't handle non-finite values.
Results may differ from a plain program's by a relative error of at most 0.012.
Values may be sent and summed in bfloat16 or wider, within the bound.
A program may use at most 256 MiB of HBM per device.

v0:
```python
import jax
import jax.numpy as jnp
from jax import lax
from jax.sharding import PartitionSpec as P

BLOCK = 128


def partner_2(block, axis, distance):
    count = lax.axis_size(axis)
    route = []
    for low in range(count):
        high = low | 1 << distance
        if high != low and high < count:
            route += [(low, high), (high, low)]
    return lax.ppermute(block, axis, route)


def turned(vector):
    half_cols = vector.shape[1] // 2
    return jnp.stack(
        [vector, jnp.concatenate([-vector[:, half_cols:], vector[:, :half_cols]], axis=1)]
    )


def forward_apply(panel_tile, vector):
    positions, width = (panel_tile.shape[2], panel_tile.shape[4])
    return lax.dot_general(
        panel_tile[:, :, :, 0, :],
        turned(vector).reshape(2, positions, width, -1),
        (((0, 2, 3), (0, 1, 2)), ((), ())),
        preferred_element_type=jnp.float32,
    )


def transposed_apply(panel_tile, vector):
    product = lax.dot_general(
        panel_tile[:, :, :, 0, :],
        turned(vector),
        (((0, 1), (0, 1)), ((), ())),
        preferred_element_type=jnp.float32,
    )
    return product.reshape(-1, vector.shape[1])


def gather_in_order(vector, order, leaf_pos):
    bit_count = len(order)
    gathered = vector[None]
    done = []
    for bit_pos in order:
        partner = partner_2(gathered, "leaf", bit_pos)
        higher = [pos for pos in done if pos > bit_pos]
        done.append(bit_pos)
        outer = 1 << len(higher)
        mine = gathered.reshape(outer, 1, -1, *vector.shape)
        theirs = partner.reshape(mine.shape)
        upper_half = leaf_pos >> bit_pos & 1 == 1
        gathered = jnp.where(
            upper_half,
            jnp.concatenate([theirs, mine], axis=1),
            jnp.concatenate([mine, theirs], axis=1),
        ).reshape(-1, *vector.shape)
    return gathered.reshape((1 << bit_count) * vector.shape[0], vector.shape[1])


def subgroup_gather(vector, bit_count, leaf_pos):
    if bit_count < 3:
        return gather_in_order(vector, list(range(bit_count))[::-1], leaf_pos)
    outer_bits = list(range(1, bit_count))
    half_cols = vector.shape[1] // 2
    first = gather_in_order(vector[:, :half_cols], outer_bits + [0], leaf_pos)
    second = gather_in_order(vector[:, half_cols:], outer_bits[::-1] + [0], leaf_pos)
    return jnp.concatenate([first, second], axis=1)


def halved_sum(total, order, leaf_pos, left):
    for bit_pos in order:
        axis = left.index(bit_pos)
        mine = leaf_pos >> bit_pos & 1
        keep = lax.dynamic_index_in_dim(total, mine, axis, keepdims=False)
        give = lax.dynamic_index_in_dim(total, 1 - mine, axis, keepdims=False)
        got = partner_2(give.astype(jnp.bfloat16), "leaf", bit_pos)
        total = keep + got.astype(jnp.float32)
        left = [pos for pos in left if pos != bit_pos]
    return total


def subgroup_sum(partial_value, bit_count, leaf_pos):
    rows = partial_value.shape[0] >> bit_count
    columns = partial_value.shape[1]
    total = partial_value.reshape((2,) * bit_count + (rows, columns))
    left = list(range(bit_count))[::-1]
    if bit_count < 3:
        return halved_sum(total, left[::-1], leaf_pos, left)
    total = halved_sum(total, [0], leaf_pos, left)
    left = left[:-1]
    half_cols = columns // 2
    first = halved_sum(total[..., :half_cols], left, leaf_pos, left)
    second = halved_sum(total[..., half_cols:], left[::-1], leaf_pos, left)
    return jnp.concatenate([first, second], axis=1)


def row_reduced(panel_tile, gathered):
    partial_value = forward_apply(panel_tile, gathered).astype(jnp.bfloat16)
    return lax.psum_scatter(partial_value, "row", scatter_dimension=0, tiled=True).astype(
        jnp.float32
    )


def row_folded(panel_tile, vector_half):
    return transposed_apply(panel_tile, lax.all_gather(vector_half, "row", axis=0, tiled=True))


def slot_ids(position, row_pos, row_size, blocks_dev, sep_blocks, has_update):
    own_slots = (position * row_size + row_pos) * blocks_dev + jnp.arange(
        blocks_dev, dtype=jnp.int32
    )
    if has_update:
        return jnp.concatenate([own_slots, own_slots + sep_blocks])
    return own_slots


def extend_add(child_rows, targets, rhs_part, bit_count, has_update, leaf_pos, row_pos, row_size):
    bit_pos = bit_count - 1
    partner_targets = partner_2(targets, "leaf", bit_pos)
    partner_rows = partner_2(child_rows.astype(jnp.bfloat16), "leaf", bit_pos).astype(jnp.float32)
    blocks_dev = targets.shape[0]
    group_size = 1 << bit_count
    position = leaf_pos & group_size - 1
    sep_blocks = group_size * row_size * blocks_dev
    slot_list = slot_ids(position, row_pos, row_size, blocks_dev, sep_blocks, has_update)
    candidates = jnp.concatenate([targets, partner_targets])
    columns = child_rows.shape[1]
    block_pool = jnp.concatenate([child_rows, partner_rows], axis=0).reshape(2 * blocks_dev, -1)
    selector = (slot_list[:, None] == candidates[None, :]).astype(jnp.float32)
    placed = jnp.dot(
        selector, block_pool, precision=lax.Precision.HIGHEST, preferred_element_type=jnp.float32
    ).reshape(-1, columns)
    slice_rows = rhs_part.shape[0]
    return (placed[:slice_rows] + rhs_part, placed[slice_rows:])


def extend_down(front_parts, targets, bit_count, leaf_pos, row_pos, row_size):
    bit_pos = bit_count - 1
    partner_parts = [
        partner_2(part.astype(jnp.bfloat16), "leaf", bit_pos).astype(jnp.float32)
        for part in front_parts
    ]
    blocks_dev = targets.shape[0]
    has_update = len(front_parts) > 1
    group_size = 1 << bit_count
    position = leaf_pos & group_size - 1
    sep_blocks = group_size * row_size * blocks_dev
    own_slots = slot_ids(position, row_pos, row_size, blocks_dev, sep_blocks, has_update)
    partner_slots = slot_ids(
        position ^ group_size // 2, row_pos, row_size, blocks_dev, sep_blocks, has_update
    )
    columns = front_parts[0].shape[1]
    block_pool = jnp.concatenate([*front_parts, *partner_parts], axis=0).reshape(
        -1, BLOCK * columns
    )
    selector = (targets[:, None] == jnp.concatenate([own_slots, partner_slots])[None, :]).astype(
        jnp.float32
    )
    return jnp.dot(
        selector, block_pool, precision=lax.Precision.HIGHEST, preferred_element_type=jnp.float32
    ).reshape(-1, columns)


def shards(leaf_update, rhs, inv_top, inv_mid, inv_low, couple_mid, couple_low, block_map):
    leaf_pos = lax.axis_index("leaf")
    row_pos = lax.axis_index("row")
    row_size = lax.axis_size("row")
    leaf_bits = lax.axis_size("leaf").bit_length() - 1
    inverses = (inv_top, inv_mid, inv_low)
    couplings = (None, couple_mid, couple_low)
    children = leaf_update
    saved_y = [None, None, None]
    for level_index in (2, 1):
        bit_count = leaf_bits - level_index
        sep_part, update_part = extend_add(
            children,
            block_map[level_index],
            rhs[level_index],
            bit_count,
            True,
            leaf_pos,
            row_pos,
            row_size,
        )
        gathered = subgroup_gather(sep_part.astype(jnp.bfloat16), bit_count, leaf_pos)
        solved = row_reduced(inverses[level_index], gathered)
        saved_y[level_index] = solved
        gathered_y = subgroup_gather(solved.astype(jnp.bfloat16), bit_count, leaf_pos)
        children = update_part - row_reduced(couplings[level_index], gathered_y)
    sep_top, unused_rows = extend_add(
        children, block_map[0], rhs[0], leaf_bits, False, leaf_pos, row_pos, row_size
    )
    gathered = subgroup_gather(sep_top.astype(jnp.bfloat16), leaf_bits, leaf_pos)
    y_top = row_reduced(inv_top, gathered)
    partial_value = row_folded(inv_top, y_top.astype(jnp.bfloat16))
    x_top = subgroup_sum(partial_value, leaf_bits, leaf_pos)
    solutions = [x_top]
    front_parts = [x_top]
    for level_index in (1, 2):
        bit_count = leaf_bits - level_index
        x_update = extend_down(
            front_parts, block_map[level_index - 1], bit_count + 1, leaf_pos, row_pos, row_size
        )
        coupled = subgroup_sum(
            row_folded(couplings[level_index], x_update.astype(jnp.bfloat16)), bit_count, leaf_pos
        )
        reduced = saved_y[level_index] - coupled
        x_sep = subgroup_sum(
            row_folded(inverses[level_index], reduced.astype(jnp.bfloat16)), bit_count, leaf_pos
        )
        solutions.append(x_sep)
        front_parts = [x_sep, x_update]
    leaf_solution = extend_down(
        front_parts, block_map[2], leaf_bits - 2, leaf_pos, row_pos, row_size
    )
    return (jnp.stack(solutions), leaf_solution)


def solution(mesh):
    return jax.shard_map(
        shards,
        mesh=mesh,
        in_specs=(
            P(("leaf", "row"), None),
            P(None, ("leaf", "row"), None),
            P(None, "leaf", None, "row", None),
            P(None, "leaf", None, "row", None),
            P(None, "leaf", None, "row", None),
            P(None, "leaf", None, "row", None),
            P(None, "leaf", None, "row", None),
            P(None, ("leaf", "row")),
        ),
        out_specs=(P(None, ("leaf", "row"), None), P(("leaf", "row"), None)),
        check_vma=False,
    )
```

profile of v0, /device:TPU:0, one launch (start us, length us, event | category | flops | bytes accessed | tf_op | source)
XLA Modules:
  0.0 577.8 jit_solution(7847423660793290802)
XLA Ops:
  15.6 6.7 %fusion.67 = bf16[2048,256]{0,1:T(8,128)(2,1)} fusion(bf16[2,2048,2,512]{3,2,1,0:T(2,128)(2,1)} %bitcast.316, bf16[1,2,512,256]{2,3,1,0:T(8,128)(2,1)S(1)} %copy.43, bf16[1,2,512,256]{2,3,1,0:T(8,128)(2,1)S(1)} %fusion.173), kind=kOutput, calls=%fused_computation.39 | convolution fusion | flops 2148532224 | bytes 10485760 | tf_op jit(solution)/shard_map/dot_general | solution.py:28
  22.4 30.0 %reduce-scatter.6.cloned.1.call-done = bf16[512,256]{0,1:T(8,128)(2,1)} async-done(((bf16[2048,256]{0,1:T(8,128)(2,1)}), bf16[512,256]{0,1:T(8,128)(2,1)}) %reduce-scatter.6.cloned.1.call-update) | async-done | bytes 262160 | tf_op jit(solution)/shard_map/reduce_scatter | solution.py:105
  57.0 6.7 %fusion.70 = bf16[2048,256]{0,1:T(8,128)(2,1)} fusion(bf16[2,2048,2,512]{3,2,1,0:T(2,128)(2,1)} %bitcast.314, bf16[1,2,512,256]{2,3,1,0:T(8,128)(2,1)S(1)} %copy.46, bf16[1,2,512,256]{2,3,1,0:T(8,128)(2,1)S(1)} %fusion.172), kind=kOutput, calls=%fused_computation.40 | convolution fusion | flops 2148532224 | bytes 10485760 | tf_op jit(solution)/shard_map/dot_general | solution.py:28
  66.1 23.6 %reduce-scatter.8.cloned.1.call-done = bf16[512,256]{0,1:T(8,128)(2,1)} async-done(((bf16[2048,256]{0,1:T(8,128)(2,1)}), bf16[512,256]{0,1:T(8,128)(2,1)}) %reduce-scatter.8.cloned.1.call-update) | async-done | bytes 262160 | tf_op jit(solution)/shard_map/reduce_scatter | solution.py:105
  92.6 5.8 %collective-permute-done.6 = bf16[512,256]{0,1:T(8,128)(2,1)S(1)} collective-permute-done((bf16[512,256]{0,1:T(8,128)(2,1)S(1)}, bf16[512,256]{0,1:T(8,128)(2,1)S(1)}, u32[]{:S(2)}, u32[]{:S(2)}) %collective-permute-start.6) | collective-permute-done | bytes 262176 | tf_op jit(solution)/shard_map/ppermute | solution.py:16
  102.1 5.3 collective-permute-done.7
  112.8 12.4 %fusion.61 = bf16[2048,256]{0,1:T(8,128)(2,1)} fusion(bf16[2,2048,4,512]{3,2,1,0:T(4,128)(2,1)} %bitcast.312, bf16[1,4,512,256]{2,3,1,0:T(8,128)(2,1)} %copy.54, bf16[1,4,512,256]{2,3,1,0:T(8,128)(2,1)S(1)} %bitcast.293), kind=kOutput, calls=%fused_computation.37 | convolution fusion | flops 4296540160 | bytes 19922944 | tf_op jit(solution)/shard_map/dot_general | solution.py:28
  125.7 26.2 %reduce-scatter.10.cloned.1.call-done = bf16[512,256]{0,1:T(8,128)(2,1)} async-done(((bf16[2048,256]{0,1:T(8,128)(2,1)}), bf16[512,256]{0,1:T(8,128)(2,1)}) %reduce-scatter.10.cloned.1.call-update) | async-done | bytes 262160 | tf_op jit(solution)/shard_map/reduce_scatter | solution.py:105
  153.4 6.4 %collective-permute-done.9 = bf16[1,512,256]{1,2,0:T(8,128)(2,1)S(1)} collective-permute-done((bf16[1,512,256]{1,2,0:T(8,128)(2,1)}, bf16[1,512,256]{1,2,0:T(8,128)(2,1)S(1)}, u32[]{:S(2)}, u32[]{:S(2)}) %collective-permute-start.9) | collective-permute-done | bytes 262176 | tf_op jit(solution)/shard_map/ppermute | solution.py:16
  165.1 12.4 %fusion.64 = bf16[2048,256]{0,1:T(8,128)(2,1)} fusion(bf16[2,2048,4,512]{3,2,1,0:T(4,128)(2,1)} %bitcast.310, bf16[1,4,512,256]{2,3,1,0:T(8,128)(2,1)} %copy.59, bf16[1,4,512,256]{2,3,1,0:T(8,128)(2,1)S(1)} %bitcast.261), kind=kOutput, calls=%fused_computation.38 | convolution fusion | flops 4296540160 | bytes 19922944 | tf_op jit(solution)/shard_map/dot_general | solution.py:28
  178.2 25.6 %reduce-scatter.12.cloned.1.call-done = bf16[512,256]{0,1:T(8,128)(2,1)} async-done(((bf16[2048,256]{0,1:T(8,128)(2,1)}), bf16[512,256]{0,1:T(8,128)(2,1)}) %reduce-scatter.12.cloned.1.call-update) | async-done | bytes 262160 | tf_op jit(solution)/shard_map/reduce_scatter | solution.py:105
  207.0 5.7 collective-permute-done
  223.9 3.9 collective-permute-done.16
  233.4 19.6 %fusion.73 = bf16[2048,256]{0,1:T(8,128)(2,1)} fusion(bf16[2,2048,8,512]{3,2,1,0:T(8,128)(2,1)} %bitcast.308, bf16[1,8,512,128]{2,3,1,0:T(8,128)(2,1)S(1)} %bitcast.287, bf16[1,8,512,128]{2,3,1,0:T(8,128)(2,1)S(1)} %neg.39, bf16[1,8,512,128]{2,3,1,0:T(8,128)(2,1)S(1)} %bitcast.263), kind=kOutput, calls=%fused_computation.41 | convolution fusion | flops 8607236096 | bytes 37748736 | tf_op jit(solution)/shard_map/dot_general | solution.py:28
  253.0 25.0 %reduce-scatter.14.cloned.1.call-done = bf16[512,256]{0,1:T(8,128)(2,1)} async-done(((bf16[2048,256]{0,1:T(8,128)(2,1)}), bf16[512,256]{0,1:T(8,128)(2,1)}) %reduce-scatter.14.cloned.1.call-update) | async-done | bytes 262160 | tf_op jit(solution)/shard_map/reduce_scatter | solution.py:105
  278.3 27.7 %all-gather.6.cloned.1.call-done = bf16[2048,256]{0,1:T(8,128)(2,1)} async-done(((bf16[512,256]{0,1:T(8,128)(2,1)}), bf16[2048,256]{0,1:T(8,128)(2,1)}) %all-gather.6.cloned.1.call-update) | async-done | bytes 1048592 | tf_op jit(solution)/shard_map/all_gather | solution.py:111
  307.5 23.9 %fusion = f32[256,8,512,1]{2,0,3,1:T(8,128)} fusion(bf16[2,2048,8,512]{3,2,1,0:T(8,128)(2,1)} %bitcast.309, bf16[1,2048,256]{1,2,0:T(8,128)(2,1)S(1)} %maximum_bitcast_fusion.14, bf16[1,2048,256]{1,2,0:T(8,128)(2,1)S(1)} %bitcast.288), kind=kOutput, calls=%fused_computation | convolution fusion | flops 8594128896 | bytes 39845888 | tf_op jit(solution)/shard_map/dot_general | solution.py:37
  333.2 2.6 collective-permute-done.18
  341.1 5.3 collective-permute-done.21
  354.6 5.2 collective-permute-done.23
  362.7 26.3 %all-gather.8.cloned.1.call-done = bf16[2048,256]{0,1:T(8,128)(2,1)} async-done(((bf16[512,256]{0,1:T(8,128)(2,1)}), bf16[2048,256]{0,1:T(8,128)(2,1)}) %all-gather.8.cloned.1.call-update) | async-done | bytes 1048592 | tf_op jit(solution)/shard_map/all_gather | solution.py:111
  390.6 8.2 %fusion.6 = f32[256,4,512,1]{2,0,3,1:T(8,128)S(1)} fusion(bf16[2,2048,4,512]{3,2,1,0:T(4,128)(2,1)} %bitcast.311, bf16[1,2048,256]{1,2,0:T(8,128)(2,1)S(1)} %maximum_bitcast_fusion.15, bf16[1,2048,256]{1,2,0:T(8,128)(2,1)S(1)} %bitcast.290), kind=kOutput, calls=%fused_computation.6 | convolution fusion | flops 4299161600 | bytes 20971520 | tf_op jit(solution)/shard_map/dot_general | solution.py:37
  407.6 6.8 %collective-permute-done.25 = bf16[512,256]{0,1:T(8,128)(2,1)S(1)} collective-permute-done((bf16[512,256]{0,1:T(8,128)(2,1)S(1)}, bf16[512,256]{0,1:T(8,128)(2,1)S(1)}, u32[]{:S(2)}, u32[]{:S(2)}) %collective-permute-start.25) | collective-permute-done | bytes 262176 | tf_op jit(solution)/shard_map/ppermute | solution.py:16
  415.3 27.5 %all-gather.10.cloned.1.call-done = bf16[2048,256]{0,1:T(8,128)(2,1)} async-done(((bf16[512,256]{0,1:T(8,128)(2,1)}), bf16[2048,256]{0,1:T(8,128)(2,1)}) %all-gather.10.cloned.1.call-update) | async-done | bytes 1048592 | tf_op jit(solution)/shard_map/all_gather | solution.py:111
  444.3 8.2 %fusion.4 = f32[256,4,512,1]{2,0,3,1:T(8,128)S(1)} fusion(bf16[2,2048,4,512]{3,2,1,0:T(4,128)(2,1)} %bitcast.313, bf16[1,2048,256]{1,2,0:T(8,128)(2,1)S(1)} %maximum_bitcast_fusion.16, bf16[1,2048,256]{1,2,0:T(8,128)(2,1)S(1)} %bitcast.289), kind=kOutput, calls=%fused_computation.4 | convolution fusion | flops 4299161600 | bytes 20971520 | tf_op jit(solution)/shard_map/dot_general | solution.py:37
  462.0 7.1 %collective-permute-done.27 = bf16[512,256]{0,1:T(8,128)(2,1)S(1)} collective-permute-done((bf16[512,256]{0,1:T(8,128)(2,1)S(1)}, bf16[512,256]{0,1:T(8,128)(2,1)S(1)}, u32[]{:S(2)}, u32[]{:S(2)}) %collective-permute-start.27) | collective-permute-done | bytes 262176 | tf_op jit(solution)/shard_map/ppermute | solution.py:16
  470.8 3.9 collective-permute-done.29
  474.7 4.6 collective-permute-done.28
  485.6 27.2 %all-gather.12.cloned.1.call-done = bf16[2048,256]{0,1:T(8,128)(2,1)} async-done(((bf16[512,256]{0,1:T(8,128)(2,1)}), bf16[2048,256]{0,1:T(8,128)(2,1)}) %all-gather.12.cloned.1.call-update) | async-done | bytes 1048592 | tf_op jit(solution)/shard_map/all_gather | solution.py:111
  514.4 5.7 fusion.94
  522.6 27.5 %all-gather.14.cloned.1.call-done = bf16[2048,256]{0,1:T(8,128)(2,1)} async-done(((bf16[512,256]{0,1:T(8,128)(2,1)}), bf16[2048,256]{0,1:T(8,128)(2,1)}) %all-gather.14.cloned.1.call-update) | async-done | bytes 1048592 | tf_op jit(solution)/shard_map/all_gather | solution.py:111
  551.7 5.7 fusion.97
  (278 shorter events, 123.1 us)
Async XLA Ops:
  7.2 45.3 %reduce-scatter.6.cloned.1.call-start = ((), (), s32[]{:S(2)}) async-start(), calls=%async_computation.5 | async-start | bytes 1310720 | tf_op jit(solution)/shard_map/reduce_scatter | solution.py:105
  22.4 67.3 %reduce-scatter.8.cloned.1.call-start = ((), (), s32[]{:S(2)}) async-start(), calls=%async_computation.6 | async-start | bytes 1310720 | tf_op jit(solution)/shard_map/reduce_scatter | solution.py:105
  63.7 88.2 %reduce-scatter.10.cloned.1.call-start = ((), (), s32[]{:S(2)}) async-start(), calls=%async_computation.7 | async-start | bytes 1310720 | tf_op jit(solution)/shard_map/reduce_scatter | solution.py:105
  64.0 28.6 %collective-permute-start.1 = (s32[4]{0:T(128)S(1)}, s32[4]{0:T(128)S(1)}, u32[]{:S(2)}, u32[]{:S(2)}) collective-permute-start(s32[4]{0:T(128)S(1)} %get-tuple-element.46), channel_id=1, source_target_pairs={{0,2},{2,0},{1,3},{3,1},{4,6},{6,4},{5,7},{7,5},{8,10},{10,8},{9,1... | collective-permute-start | bytes 56 | tf_op jit(solution)/shard_map/ppermute | solution.py:16
  90.7 7.7 %collective-permute-start.6 = (bf16[512,256]{0,1:T(8,128)(2,1)S(1)}, bf16[512,256]{0,1:T(8,128)(2,1)S(1)}, u32[]{:S(2)}, u32[]{:S(2)}) collective-permute-start(bf16[512,256]{0,1:T(8,128)(2,1)S(1)} %get-tuple-element.12), channel_id=1, source_target_pairs={{0,2},{2,0},{1,3},{3,1},{4,6},{6,4},{5,7},{7,5},{8,10},{10,8},{9,1... | collective-permute-start | bytes 786440 | tf_op jit(solution)/shard_map/ppermute | solution.py:16
  100.6 6.9 %collective-permute-start.7 = (bf16[1,512,256]{1,2,0:T(8,128)(2,1)S(1)}, bf16[1,512,256]{1,2,0:T(8,128)(2,1)S(1)}, u32[]{:S(2)}, u32[]{:S(2)}) collective-permute-start(bf16[1,512,256]{1,2,0:T(8,128)(2,1)S(1)} %add_convert_fusion), channel_id=1, source_target_pairs={{0,2},{2,0},{1,3},{3,1},{4,6},{6,4},{5,7},{7,5},{8,10},{10,8},{9,1... | collective-permute-start | bytes 786440 | tf_op jit(solution)/shard_map/ppermute | solution.py:16
  125.3 78.6 %reduce-scatter.12.cloned.1.call-start = ((), (), s32[]{:S(2)}) async-start(), calls=%async_computation.8 | async-start | bytes 1310720 | tf_op jit(solution)/shard_map/reduce_scatter | solution.py:105
  151.9 7.9 %collective-permute-start.9 = (bf16[1,512,256]{1,2,0:T(8,128)(2,1)}, bf16[1,512,256]{1,2,0:T(8,128)(2,1)S(1)}, u32[]{:S(2)}, u32[]{:S(2)}) collective-permute-start(bf16[1,512,256]{1,2,0:T(8,128)(2,1)} %bitcast.277), channel_id=1, source_target_pairs={{0,2},{2,0},{1,3},{3,1},{4,6},{6,4},{5,7},{7,5},{8,10},{10,8},{9,1... | collective-permute-start | bytes 786440 | tf_op jit(solution)/shard_map/ppermute | solution.py:16
  177.6 100.4 %reduce-scatter.14.cloned.1.call-start = ((), (), s32[]{:S(2)}) async-start(), calls=%async_computation.9 | async-start | bytes 1310720 | tf_op jit(solution)/shard_map/reduce_scatter | solution.py:105
  204.9 7.9 %collective-permute-start.11 = (bf16[512,256]{0,1:T(8,128)(2,1)S(1)}, bf16[512,256]{0,1:T(8,128)(2,1)S(1)}, u32[]{:S(2)}, u32[]{:S(2)}) collective-permute-start(bf16[512,256]{0,1:T(8,128)(2,1)S(1)} %get-tuple-element.10), channel_id=1, source_target_pairs={{0,4},{4,0},{1,5},{5,1},{2,6},{6,2},{3,7},{7,3},{8,12},{12,8},{9,1... | collective-permute-start | bytes 786440 | tf_op jit(solution)/shard_map/ppermute | solution.py:16
  206.5 6.3 %collective-permute-start = (s32[4]{0:T(128)S(1)}, s32[4]{0:T(128)S(1)}, u32[]{:S(2)}, u32[]{:S(2)}) collective-permute-start(s32[4]{0:T(128)S(1)} %get-tuple-element.44), channel_id=1, source_target_pairs={{0,4},{4,0},{1,5},{5,1},{2,6},{6,2},{3,7},{7,3},{8,12},{12,8},{9,1... | collective-permute-start | bytes 56 | tf_op jit(solution)/shard_map/ppermute | solution.py:16
  215.7 5.0 collective-permute-start.15
  217.2 6.4 %collective-permute-start.12 = (bf16[1,512,128]{2,1,0:T(8,128)(2,1)S(1)}, bf16[1,512,128]{2,1,0:T(8,128)(2,1)S(1)}, u32[]{:S(2)}, u32[]{:S(2)}) collective-permute-start(bf16[1,512,128]{2,1,0:T(8,128)(2,1)S(1)} %get-tuple-element.43), channel_id=1, source_target_pairs={{0,2},{2,0},{1,3},{3,1},{4,6},{6,4},{5,7},{7,5},{8,10},{10,8},{9,1... | collective-permute-start | bytes 393224 | tf_op jit(solution)/shard_map/ppermute | solution.py:16
  220.8 7.0 %collective-permute-start.16 = (bf16[2,512,128]{2,1,0:T(8,128)(2,1)S(1)}, bf16[2,512,128]{2,1,0:T(8,128)(2,1)S(1)}, u32[]{:S(2)}, u32[]{:S(2)}) collective-permute-start(bf16[2,512,128]{2,1,0:T(8,128)(2,1)S(1)} %maximum_select_fusion.13), channel_id=1, source_target_pairs={{0,2},{2,0},{1,3},{3,1},{4,6},{6,4},{5,7},{7,5},{8,10},{10,8},{9,1... | collective-permute-start | bytes 786440 | tf_op jit(solution)/shard_map/ppermute | solution.py:16
  223.6 6.4 %collective-permute-start.13 = (bf16[2,512,128]{2,1,0:T(8,128)(2,1)S(1)}, bf16[2,512,128]{2,1,0:T(8,128)(2,1)S(1)}, u32[]{:S(2)}, u32[]{:S(2)}) collective-permute-start(bf16[2,512,128]{2,1,0:T(8,128)(2,1)S(1)} %maximum_select_fusion.11), channel_id=1, source_target_pairs={{0,4},{4,0},{1,5},{5,1},{2,6},{6,2},{3,7},{7,3},{8,12},{12,8},{9,1... | collective-permute-start | bytes 786440 | tf_op jit(solution)/shard_map/ppermute | solution.py:16
  228.1 3.5 collective-permute-start.17
  253.0 53.0 %all-gather.6.cloned.1.call-start = ((), (), s32[]{:S(2)}) async-start(), calls=%async_computation.10 | async-start | bytes 1310720 | tf_op jit(solution)/shard_map/all_gather | solution.py:111
  278.1 111.0 %all-gather.8.cloned.1.call-start = ((), (), s32[]{:S(2)}) async-start(), calls=%async_computation.11 | async-start | bytes 1310720 | tf_op jit(solution)/shard_map/all_gather | solution.py:111
  338.0 8.4 %collective-permute-start.21 = (bf16[2,512,128]{1,2,0:T(8,128)(2,1)S(1)}, bf16[2,512,128]{1,2,0:T(8,128)(2,1)S(1)}, u32[]{:S(2)}, u32[]{:S(2)}) collective-permute-start(bf16[2,512,128]{1,2,0:T(8,128)(2,1)S(1)} %fusion.117), channel_id=1, source_target_pairs={{0,2},{2,0},{1,3},{3,1},{4,6},{6,4},{5,7},{7,5},{8,10},{10,8},{9,1... | collective-permute-start | bytes 786440 | tf_op jit(solution)/shard_map/ppermute | solution.py:16
  339.6 8.5 %collective-permute-start.19 = (bf16[2,512,128]{1,2,0:T(8,128)(2,1)S(1)}, bf16[2,512,128]{1,2,0:T(8,128)(2,1)S(1)}, u32[]{:S(2)}, u32[]{:S(2)}) collective-permute-start(bf16[2,512,128]{1,2,0:T(8,128)(2,1)S(1)} %fusion.116), channel_id=1, source_target_pairs={{0,4},{4,0},{1,5},{5,1},{2,6},{6,2},{3,7},{7,3},{8,12},{12,8},{9,1... | collective-permute-start | bytes 786440 | tf_op jit(solution)/shard_map/ppermute | solution.py:16
  346.5 5.0 collective-permute-start.22
  348.2 5.0 collective-permute-start.20
  353.3 6.4 %collective-permute-start.23 = (bf16[512,256]{0,1:T(8,128)(2,1)S(1)}, bf16[512,256]{0,1:T(8,128)(2,1)S(1)}, u32[]{:S(2)}, u32[]{:S(2)}) collective-permute-start(bf16[512,256]{0,1:T(8,128)(2,1)S(1)} %fusion.114), channel_id=1, source_target_pairs={{0,4},{4,0},{1,5},{5,1},{2,6},{6,2},{3,7},{7,3},{8,12},{12,8},{9,1... | collective-permute-start | bytes 786440 | tf_op jit(solution)/shard_map/ppermute | solution.py:16
  362.4 80.3 %all-gather.10.cloned.1.call-start = ((), (), s32[]{:S(2)}) async-start(), calls=%async_computation.12 | async-start | bytes 1310720 | tf_op jit(solution)/shard_map/all_gather | solution.py:111
  399.7 5.0 collective-permute-start.24
  406.1 8.3 %collective-permute-start.25 = (bf16[512,256]{0,1:T(8,128)(2,1)S(1)}, bf16[512,256]{0,1:T(8,128)(2,1)S(1)}, u32[]{:S(2)}, u32[]{:S(2)}) collective-permute-start(bf16[512,256]{0,1:T(8,128)(2,1)S(1)} %fusion.118), channel_id=1, source_target_pairs={{0,2},{2,0},{1,3},{3,1},{4,6},{6,4},{5,7},{7,5},{8,10},{10,8},{9,1... | collective-permute-start | bytes 786440 | tf_op jit(solution)/shard_map/ppermute | solution.py:16
  415.2 97.6 %all-gather.12.cloned.1.call-start = ((), (), s32[]{:S(2)}) async-start(), calls=%async_computation.13 | async-start | bytes 1310720 | tf_op jit(solution)/shard_map/all_gather | solution.py:111
  453.4 5.1 collective-permute-start.26
  459.8 9.2 %collective-permute-start.27 = (bf16[512,256]{0,1:T(8,128)(2,1)S(1)}, bf16[512,256]{0,1:T(8,128)(2,1)S(1)}, u32[]{:S(2)}, u32[]{:S(2)}) collective-permute-start(bf16[512,256]{0,1:T(8,128)(2,1)S(1)} %fusion.119), channel_id=1, source_target_pairs={{0,2},{2,0},{1,3},{3,1},{4,6},{6,4},{5,7},{7,5},{8,10},{10,8},{9,1... | collective-permute-start | bytes 786440 | tf_op jit(solution)/shard_map/ppermute | solution.py:16
  461.3 13.3 %collective-permute-start.29 = (bf16[512,256]{0,1:T(8,128)(2,1)S(1)}, bf16[512,256]{0,1:T(8,128)(2,1)S(1)}, u32[]{:S(2)}, u32[]{:S(2)}) collective-permute-start(bf16[512,256]{0,1:T(8,128)(2,1)S(1)} %copy-done.7), channel_id=1, source_target_pairs={{0,2},{2,0},{1,3},{3,1},{4,6},{6,4},{5,7},{7,5},{8,10},{10,8},{9,1... | collective-permute-start | bytes 786440 | tf_op jit(solution)/shard_map/ppermute | solution.py:16
  469.1 10.2 %collective-permute-start.28 = (bf16[512,256]{0,1:T(8,128)(2,1)S(1)}, bf16[512,256]{0,1:T(8,128)(2,1)S(1)}, u32[]{:S(2)}, u32[]{:S(2)}) collective-permute-start(bf16[512,256]{0,1:T(8,128)(2,1)S(1)} %get-tuple-element.8), channel_id=1, source_target_pairs={{0,2},{2,0},{1,3},{3,1},{4,6},{6,4},{5,7},{7,5},{8,10},{10,8},{9,1... | collective-permute-start | bytes 786440 | tf_op jit(solution)/shard_map/ppermute | solution.py:16
  485.3 64.8 %all-gather.14.cloned.1.call-start = ((), (), s32[]{:S(2)}) async-start(), calls=%async_computation.14 | async-start | bytes 1310720 | tf_op jit(solution)/shard_map/all_gather | solution.py:111
  (33 other events, 106.8 us)
Sparse Core Ops, SparseCore 0:
  22.5 29.8 reduce-scatter.5
  63.8 25.7 reduce-scatter.7
  125.4 26.4 reduce-scatter.9
  177.7 26.0 reduce-scatter.11
  253.1 24.8 reduce-scatter.13
  279.5 26.4 all-gather.5
  362.6 26.4 all-gather.7
  415.3 27.3 all-gather.9
  485.4 27.3 all-gather.11
  522.7 27.3 all-gather.13
where the time goes:
time: 585 us; the launch traced here: 578 us
  waiting for transfers between devices  348 us (59%)
  matrix products  114 us (19%)
  local copies, waits for them, and re-layouts  40.2 us (7%)
  other arithmetic  31.2 us (5%)
  starting transfers between devices  29.3 us (5%)
  between operations  15.8 us (3%)
    all_gather x5, waiting for transfers between devices, row_folded(): lax.all_gather(vector_half, 'row', axis=0, tiled=True)  136 us
    reduce_scatter x5, waiting for transfers between devices, row_reduced(): lax.psum_scatter(partial_value, 'row', scatter_dimension=0, tiled=True)  130 us
    ppermute x34, waiting for transfers between devices, partner_2(): return lax.ppermute(block, axis, route)  80.7 us
    dot_general x5, matrix products, forward_apply(): lax.dot_general(panel_tile[:, :, :, 0, :], turned(vector).reshape(2, posi...  57.9 us
    dot_general x5, matrix products, transposed_apply(): lax.dot_general(panel_tile[:, :, :, 0, :], turned(vector), (((0, 1), (0,...  51.7 us
    ppermute x34, starting transfers between devices, partner_2(): return lax.ppermute(block, axis, route)  27.6 us
  transfers between devices with their start and end apart: 44, of which 34 were waited for; matrix products, arithmetic and copies ran while one was open for 4% of the time, Pallas kernels for 0%

commit v1 on v0

--- a/solution.py
+++ b/solution.py
@@ -2,8 +2,32 @@
 import jax.numpy as jnp
 from jax import lax
 from jax.sharding import PartitionSpec as P
+from jax.lax import axis_index, axis_size, ppermute
 
 BLOCK = 128
+
+
+def connect_hubs(my_data):
+    all_values = axis_index("row")
+    current_value = axis_size("row")
+    state_next, arr_out, w1 = (current_value, all_values, my_data.shape[0])
+    nodes = [dev_i * state_next if k == 0 else dev_i for k, dev_i in enumerate(my_data.shape)]
+    v_next = jnp.zeros(nodes, my_data.dtype)
+    field_out = newest = my_data
+    side_arr = lax.dynamic_update_slice_in_dim(v_next, my_data, arr_out * w1, axis=0)
+    for tick in range(1, state_next // 2 + 1):
+        field_out = ppermute(
+            field_out, "row", perm=[(k, (k + 1) % state_next) for k in range(state_next)]
+        )
+        side_arr = lax.dynamic_update_slice_in_dim(
+            side_arr, field_out, (arr_out - tick) % state_next * w1, axis=0
+        )
+        if 2 * tick < state_next:
+            newest = ppermute(newest, "row", [(k, (k - 1) % state_next) for k in range(state_next)])
+            side_arr = lax.dynamic_update_slice_in_dim(
+                side_arr, newest, (arr_out + tick) % state_next * w1, axis=0
+            )
+    return side_arr
 
 
 def partner_2(block, axis, distance):
@@ -108,7 +132,7 @@
 
 
 def row_folded(panel_tile, vector_half):
-    return transposed_apply(panel_tile, lax.all_gather(vector_half, "row", axis=0, tiled=True))
+    return transposed_apply(panel_tile, connect_hubs(vector_half))
 
 
 def slot_ids(position, row_pos, row_size, blocks_dev, sep_blocks, has_update):

time: 585 us -> 545 us (0.932)
  waiting for transfers between devices: 348 us -> 291 us
  starting transfers between devices: 29.3 us -> 47.9 us
  local copies, waits for them, and re-layouts: 40.2 us -> 52.9 us
  other arithmetic: 31.2 us -> 19.4 us
    all_gather x5 -> x0, waiting for transfers between devices: 136 us -> none  [row_folded(): lax.all_gather(vector_half, 'row', axis=0, tiled=True)]
    ppermute x0 -> x15, waiting for transfers between devices: none -> 81.4 us  [the longest x10 71.8 us: connect_hubs(): ppermute(field_out, 'row', perm=[(k, (k + 1) % state_next) for k in range...]
    ppermute x0 -> x15, starting transfers between devices: none -> 19.9 us  [the longest x5 19.1 us: connect_hubs(): ppermute(newest, 'row', [(k, (k - 1) % state_next) for k in range(state_n...]
    neg x10, other arithmetic: 7.37 us -> 0.94 us  [turned(): -vector[:, half_cols:]]
  transfers between devices with their start and end apart: 44 -> 54, of which waited for: 34 -> 43; matrix products, arithmetic and copies ran while one was open for 4% -> 6% of each run, Pallas kernels for 0% -> 0%
where the time goes in v1:
time: 545 us; the launch traced here: 538 us
  waiting for transfers between devices  291 us (53%)
  matrix products  111 us (20%)
  local copies, waits for them, and re-layouts  52.9 us (10%)
  starting transfers between devices  47.9 us (9%)
  other arithmetic  19.4 us (4%)
  between operations  15.7 us (3%)
    reduce_scatter x5, waiting for transfers between devices, row_reduced(): lax.psum_scatter(partial_value, 'row', scatter_dimension=0, tiled=True)  131 us
    ppermute x34, waiting for transfers between devices, partner_2(): return lax.ppermute(block, axis, route)  79.2 us
    ppermute x10, waiting for transfers between devices, connect_hubs(): ppermute(field_out, 'row', perm=[(k, (k + 1) % state_next) for k in range...  71.8 us
    dot_general x5, matrix products, forward_apply(): lax.dot_general(panel_tile[:, :, :, 0, :], turned(vector).reshape(2, posi...  57.9 us
    dot_general x5, matrix products, transposed_apply(): lax.dot_general(panel_tile[:, :, :, 0, :], turned(vector), (((0, 1), (0,...  48.5 us
    ppermute x34, starting transfers between devices, partner_2(): return lax.ppermute(block, axis, route)  27.2 us
    ppermute x5, starting transfers between devices, connect_hubs(): ppermute(newest, 'row', [(k, (k - 1) % state_next) for k in range(state_n...  19.1 us
  transfers between devices with their start and end apart: 54, of which 43 were waited for; matrix products, arithmetic and copies ran while one was open for 6% of the time, Pallas kernels for 0%

profile of v1, /device:TPU:0, one launch (start us, length us, event | category | flops | bytes accessed | tf_op | source)
XLA Modules:
  0.0 537.7 jit_solution(9571968614454887647)
XLA Ops:
  15.6 6.7 %fusion.67 = bf16[2048,256]{0,1:T(8,128)(2,1)} fusion(bf16[2,2048,2,512]{3,2,1,0:T(2,128)(2,1)} %bitcast.320, bf16[1,2,512,256]{2,3,1,0:T(8,128)(2,1)S(1)} %copy.39, bf16[1,2,512,256]{2,3,1,0:T(8,128)(2,1)S(1)} %fusion.175), kind=kOutput, calls=%fused_computation.39 | convolution fusion | flops 2148532224 | bytes 10485760 | tf_op jit(solution)/shard_map/dot_general | solution.py:52
  22.4 30.0 %reduce-scatter.6.cloned.1.call-done = bf16[512,256]{0,1:T(8,128)(2,1)} async-done(((bf16[2048,256]{0,1:T(8,128)(2,1)}), bf16[512,256]{0,1:T(8,128)(2,1)}) %reduce-scatter.6.cloned.1.call-update) | async-done | bytes 262160 | tf_op jit(solution)/shard_map/reduce_scatter | solution.py:129
  57.0 6.7 %fusion.70 = bf16[2048,256]{0,1:T(8,128)(2,1)} fusion(bf16[2,2048,2,512]{3,2,1,0:T(2,128)(2,1)} %bitcast.318, bf16[1,2,512,256]{2,3,1,0:T(8,128)(2,1)S(1)} %copy.42, bf16[1,2,512,256]{2,3,1,0:T(8,128)(2,1)S(1)} %fusion.174), kind=kOutput, calls=%fused_computation.40 | convolution fusion | flops 2148532224 | bytes 10485760 | tf_op jit(solution)/shard_map/dot_general | solution.py:52
  66.1 23.6 %reduce-scatter.8.cloned.1.call-done = bf16[512,256]{0,1:T(8,128)(2,1)} async-done(((bf16[2048,256]{0,1:T(8,128)(2,1)}), bf16[512,256]{0,1:T(8,128)(2,1)}) %reduce-scatter.8.cloned.1.call-update) | async-done | bytes 262160 | tf_op jit(solution)/shard_map/reduce_scatter | solution.py:129
  92.6 5.8 %collective-permute-done.6 = bf16[512,256]{0,1:T(8,128)(2,1)S(1)} collective-permute-done((bf16[512,256]{0,1:T(8,128)(2,1)S(1)}, bf16[512,256]{0,1:T(8,128)(2,1)S(1)}, u32[]{:S(2)}, u32[]{:S(2)}) %collective-permute-start.6) | collective-permute-done | bytes 262176 | tf_op jit(solution)/shard_map/ppermute | solution.py:40
  102.1 5.3 collective-permute-done.7
  112.8 12.4 %fusion.61 = bf16[2048,256]{0,1:T(8,128)(2,1)} fusion(bf16[2,2048,4,512]{3,2,1,0:T(4,128)(2,1)} %bitcast.316, bf16[1,4,512,256]{2,3,1,0:T(8,128)(2,1)} %copy.50, bf16[1,4,512,256]{2,3,1,0:T(8,128)(2,1)S(1)} %bitcast.297), kind=kOutput, calls=%fused_computation.37 | convolution fusion | flops 4296540160 | bytes 19922944 | tf_op jit(solution)/shard_map/dot_general | solution.py:52
  125.7 26.2 %reduce-scatter.10.cloned.1.call-done = bf16[512,256]{0,1:T(8,128)(2,1)} async-done(((bf16[2048,256]{0,1:T(8,128)(2,1)}), bf16[512,256]{0,1:T(8,128)(2,1)}) %reduce-scatter.10.cloned.1.call-update) | async-done | bytes 262160 | tf_op jit(solution)/shard_map/reduce_scatter | solution.py:129
  153.4 6.4 %collective-permute-done.9 = bf16[1,512,256]{1,2,0:T(8,128)(2,1)S(1)} collective-permute-done((bf16[1,512,256]{1,2,0:T(8,128)(2,1)}, bf16[1,512,256]{1,2,0:T(8,128)(2,1)S(1)}, u32[]{:S(2)}, u32[]{:S(2)}) %collective-permute-start.9) | collective-permute-done | bytes 262176 | tf_op jit(solution)/shard_map/ppermute | solution.py:40
  165.1 12.4 %fusion.64 = bf16[2048,256]{0,1:T(8,128)(2,1)} fusion(bf16[2,2048,4,512]{3,2,1,0:T(4,128)(2,1)} %bitcast.314, bf16[1,4,512,256]{2,3,1,0:T(8,128)(2,1)} %copy.55, bf16[1,4,512,256]{2,3,1,0:T(8,128)(2,1)S(1)} %bitcast.267), kind=kOutput, calls=%fused_computation.38 | convolution fusion | flops 4296540160 | bytes 19922944 | tf_op jit(solution)/shard_map/dot_general | solution.py:52
  178.2 25.7 %reduce-scatter.12.cloned.1.call-done = bf16[512,256]{0,1:T(8,128)(2,1)} async-done(((bf16[2048,256]{0,1:T(8,128)(2,1)}), bf16[512,256]{0,1:T(8,128)(2,1)}) %reduce-scatter.12.cloned.1.call-update) | async-done | bytes 262160 | tf_op jit(solution)/shard_map/reduce_scatter | solution.py:129
  207.0 5.7 %collective-permute-done = s32[4]{0:T(128)S(1)} collective-permute-done((s32[4]{0:T(128)S(1)}, s32[4]{0:T(128)S(1)}, u32[]{:S(2)}, u32[]{:S(2)}) %collective-permute-start) | collective-permute-done | bytes 48 | tf_op jit(solution)/shard_map/ppermute | solution.py:40
  233.4 19.6 %fusion.73 = bf16[2048,256]{0,1:T(8,128)(2,1)} fusion(bf16[2,2048,8,512]{3,2,1,0:T(8,128)(2,1)} %bitcast.312, bf16[1,8,512,128]{2,3,1,0:T(8,128)(2,1)S(1)} %bitcast.296, bf16[1,8,512,128]{2,3,1,0:T(8,128)(2,1)S(1)} %neg.39, bf16[1,8,512,128]{2,3,1,0:T(8,128)(2,1)S(1)} %bitcast.269), kind=kOutput, calls=%fused_computation.41 | convolution fusion | flops 8607236096 | bytes 37748736 | tf_op jit(solution)/shard_map/dot_general | solution.py:52
  253.0 25.1 %reduce-scatter.14.cloned.1.call-done = bf16[512,256]{0,1:T(8,128)(2,1)} async-done(((bf16[2048,256]{0,1:T(8,128)(2,1)}), bf16[512,256]{0,1:T(8,128)(2,1)}) %reduce-scatter.14.cloned.1.call-update) | async-done | bytes 262160 | tf_op jit(solution)/shard_map/reduce_scatter | solution.py:129
  281.9 7.4 %collective-permute-done.18 = bf16[512,256]{0,1:T(8,128)(2,1)S(1)} collective-permute-done((bf16[512,256]{0,1:T(8,128)(2,1)}, bf16[512,256]{0,1:T(8,128)(2,1)S(1)}, u32[]{:S(2)}, u32[]{:S(2)}) %collective-permute-start.18) | collective-permute-done | bytes 262176 | tf_op jit(solution)/shard_map/ppermute | solution.py:19
  291.6 7.4 %collective-permute-done.20 = bf16[512,256]{0,1:T(8,128)(2,1)S(1)} collective-permute-done((bf16[512,256]{0,1:T(8,128)(2,1)S(1)}, bf16[512,256]{0,1:T(8,128)(2,1)S(1)}, u32[]{:S(2)}, u32[]{:S(2)}) %collective-permute-start.20) | collective-permute-done | bytes 262176 | tf_op jit(solution)/shard_map/ppermute | solution.py:19
  299.2 23.9 %fusion = f32[256,8,512,1]{2,0,3,1:T(8,128)} fusion(bf16[2,2048,8,512]{3,2,1,0:T(8,128)(2,1)} %bitcast.313, bf16[1,2048,256]{1,2,0:T(8,128)(2,1)S(1)} %maximum_bitcast_fusion.14, bf16[1,2048,256]{1,2,0:T(8,128)(2,1)S(1)} %bitcast.278), kind=kOutput, calls=%fused_computation | convolution fusion | flops 8594128896 | bytes 39845888 | tf_op jit(solution)/shard_map/dot_general | solution.py:61
  325.8 5.4 copy.67
  339.9 5.7 %collective-permute-done.22 = bf16[2,512,128]{1,2,0:T(8,128)(2,1)S(1)} collective-permute-done((bf16[2,512,128]{1,2,0:T(8,128)(2,1)S(1)}, bf16[2,512,128]{1,2,0:T(8,128)(2,1)S(1)}, u32[]{:S(2)}, u32[]{:S(2)}) %collective-permute-start.22) | collective-permute-done | bytes 262176 | tf_op jit(solution)/shard_map/ppermute | solution.py:40
  365.2 7.2 %collective-permute-done.27 = bf16[512,256]{0,1:T(8,128)(2,1)S(1)} collective-permute-done((bf16[512,256]{0,1:T(8,128)(2,1)S(1)}, bf16[512,256]{0,1:T(8,128)(2,1)S(1)}, u32[]{:S(2)}, u32[]{:S(2)}) %collective-permute-start.27) | collective-permute-done | bytes 262176 | tf_op jit(solution)/shard_map/ppermute | solution.py:19
  374.5 6.3 %collective-permute-done.29 = bf16[512,256]{0,1:T(8,128)(2,1)S(1)} collective-permute-done((bf16[512,256]{0,1:T(8,128)(2,1)S(1)}, bf16[512,256]{0,1:T(8,128)(2,1)S(1)}, u32[]{:S(2)}, u32[]{:S(2)}) %collective-permute-start.29) | collective-permute-done | bytes 262176 | tf_op jit(solution)/shard_map/ppermute | solution.py:19
  380.9 8.2 %fusion.6 = f32[256,4,512,1]{2,0,3,1:T(8,128)S(1)} fusion(bf16[2,2048,4,512]{3,2,1,0:T(4,128)(2,1)} %bitcast.315, bf16[1,2048,256]{1,2,0:T(8,128)(2,1)S(1)} %maximum_bitcast_fusion.15, bf16[1,2048,256]{1,2,0:T(8,128)(2,1)S(1)} %bitcast.276), kind=kOutput, calls=%fused_computation.6 | convolution fusion | flops 4299161600 | bytes 20971520 | tf_op jit(solution)/shard_map/dot_general | solution.py:61
  397.6 7.1 %collective-permute-done.31 = bf16[512,256]{0,1:T(8,128)(2,1)S(1)} collective-permute-done((bf16[512,256]{0,1:T(8,128)(2,1)S(1)}, bf16[512,256]{0,1:T(8,128)(2,1)S(1)}, u32[]{:S(2)}, u32[]{:S(2)}) %collective-permute-start.31) | collective-permute-done | bytes 262176 | tf_op jit(solution)/shard_map/ppermute | solution.py:40
  408.9 7.2 %collective-permute-done.32 = bf16[512,256]{0,1:T(8,128)(2,1)S(1)} collective-permute-done((bf16[512,256]{0,1:T(8,128)(2,1)S(1)}, bf16[512,256]{0,1:T(8,128)(2,1)S(1)}, u32[]{:S(2)}, u32[]{:S(2)}) %collective-permute-start.32) | collective-permute-done | bytes 262176 | tf_op jit(solution)/shard_map/ppermute | solution.py:19
  418.1 7.4 %collective-permute-done.34 = bf16[512,256]{0,1:T(8,128)(2,1)S(1)} collective-permute-done((bf16[512,256]{0,1:T(8,128)(2,1)S(1)}, bf16[512,256]{0,1:T(8,128)(2,1)S(1)}, u32[]{:S(2)}, u32[]{:S(2)}) %collective-permute-start.34) | collective-permute-done | bytes 262176 | tf_op jit(solution)/shard_map/ppermute | solution.py:19
  425.7 8.2 %fusion.4 = f32[256,4,512,1]{2,0,3,1:T(8,128)S(1)} fusion(bf16[2,2048,4,512]{3,2,1,0:T(4,128)(2,1)} %bitcast.317, bf16[1,2048,256]{1,2,0:T(8,128)(2,1)S(1)} %maximum_bitcast_fusion.16, bf16[1,2048,256]{1,2,0:T(8,128)(2,1)S(1)} %bitcast.271), kind=kOutput, calls=%fused_computation.4 | convolution fusion | flops 4299161600 | bytes 20971520 | tf_op jit(solution)/shard_map/dot_general | solution.py:61
  442.3 7.1 %collective-permute-done.36 = bf16[512,256]{0,1:T(8,128)(2,1)S(1)} collective-permute-done((bf16[512,256]{0,1:T(8,128)(2,1)S(1)}, bf16[512,256]{0,1:T(8,128)(2,1)S(1)}, u32[]{:S(2)}, u32[]{:S(2)}) %collective-permute-start.36) | collective-permute-done | bytes 262176 | tf_op jit(solution)/shard_map/ppermute | solution.py:40
  469.0 7.2 %collective-permute-done.39 = bf16[512,256]{0,1:T(8,128)(2,1)S(1)} collective-permute-done((bf16[512,256]{0,1:T(8,128)(2,1)S(1)}, bf16[512,256]{0,1:T(8,128)(2,1)S(1)}, u32[]{:S(2)}, u32[]{:S(2)}) %collective-permute-start.39) | collective-permute-done | bytes 262176 | tf_op jit(solution)/shard_map/ppermute | solution.py:19
  478.2 7.4 %collective-permute-done.41 = bf16[512,256]{0,1:T(8,128)(2,1)S(1)} collective-permute-done((bf16[512,256]{0,1:T(8,128)(2,1)S(1)}, bf16[512,256]{0,1:T(8,128)(2,1)S(1)}, u32[]{:S(2)}, u32[]{:S(2)}) %collective-permute-start.41) | collective-permute-done | bytes 262176 | tf_op jit(solution)/shard_map/ppermute | solution.py:19
  485.8 5.9 %fusion.94 = f32[256,2,512]{2,0,1:T(8,128)S(1)} fusion(bf16[2,2048,2,512]{3,2,1,0:T(2,128)(2,1)} %bitcast.319, bf16[1,2048,256]{1,2,0:T(8,128)(2,1)S(1)} %maximum_bitcast_fusion.17, bf16[1,2048,256]{1,2,0:T(8,128)(2,1)S(1)} %bitcast.277), kind=kOutput, calls=%fused_computation.68 | convolution fusion | flops 2151677952 | bytes 11534336 | tf_op jit(solution)/shard_map/dot_general | solution.py:61
  497.5 7.2 %collective-permute-done.43 = bf16[512,256]{0,1:T(8,128)(2,1)S(1)} collective-permute-done((bf16[512,256]{0,1:T(8,128)(2,1)S(1)}, bf16[512,256]{0,1:T(8,128)(2,1)S(1)}, u32[]{:S(2)}, u32[]{:S(2)}) %collective-permute-start.43) | collective-permute-done | bytes 262176 | tf_op jit(solution)/shard_map/ppermute | solution.py:19
  507.7 7.4 %collective-permute-done.45 = bf16[512,256]{0,1:T(8,128)(2,1)S(1)} collective-permute-done((bf16[512,256]{0,1:T(8,128)(2,1)S(1)}, bf16[512,256]{0,1:T(8,128)(2,1)S(1)}, u32[]{:S(2)}, u32[]{:S(2)}) %collective-permute-start.45) | collective-permute-done | bytes 262176 | tf_op jit(solution)/shard_map/ppermute | solution.py:19
  (314 shorter events, 167.1 us)
Async XLA Ops:
  7.2 45.3 %reduce-scatter.6.cloned.1.call-start = ((), (), s32[]{:S(2)}) async-start(), calls=%async_computation.5 | async-start | bytes 1310720 | tf_op jit(solution)/shard_map/reduce_scatter | solution.py:129
  22.4 67.3 %reduce-scatter.8.cloned.1.call-start = ((), (), s32[]{:S(2)}) async-start(), calls=%async_computation.6 | async-start | bytes 1310720 | tf_op jit(solution)/shard_map/reduce_scatter | solution.py:129
  63.7 88.2 %reduce-scatter.10.cloned.1.call-start = ((), (), s32[]{:S(2)}) async-start(), calls=%async_computation.7 | async-start | bytes 1310720 | tf_op jit(solution)/shard_map/reduce_scatter | solution.py:129
  64.0 28.6 %collective-permute-start.1 = (s32[4]{0:T(128)S(1)}, s32[4]{0:T(128)S(1)}, u32[]{:S(2)}, u32[]{:S(2)}) collective-permute-start(s32[4]{0:T(128)S(1)} %get-tuple-element.54), channel_id=1, source_target_pairs={{0,2},{2,0},{1,3},{3,1},{4,6},{6,4},{5,7},{7,5},{8,10},{10,8},{9,1... | collective-permute-start | bytes 56 | tf_op jit(solution)/shard_map/ppermute | solution.py:40
  90.7 7.7 %collective-permute-start.6 = (bf16[512,256]{0,1:T(8,128)(2,1)S(1)}, bf16[512,256]{0,1:T(8,128)(2,1)S(1)}, u32[]{:S(2)}, u32[]{:S(2)}) collective-permute-start(bf16[512,256]{0,1:T(8,128)(2,1)S(1)} %get-tuple-element.20), channel_id=1, source_target_pairs={{0,2},{2,0},{1,3},{3,1},{4,6},{6,4},{5,7},{7,5},{8,10},{10,8},{9,1... | collective-permute-start | bytes 786440 | tf_op jit(solution)/shard_map/ppermute | solution.py:40
  125.3 78.6 %reduce-scatter.12.cloned.1.call-start = ((), (), s32[]{:S(2)}) async-start(), calls=%async_computation.8 | async-start | bytes 1310720 | tf_op jit(solution)/shard_map/reduce_scatter | solution.py:129
  151.9 7.9 %collective-permute-start.9 = (bf16[1,512,256]{1,2,0:T(8,128)(2,1)}, bf16[1,512,256]{1,2,0:T(8,128)(2,1)S(1)}, u32[]{:S(2)}, u32[]{:S(2)}) collective-permute-start(bf16[1,512,256]{1,2,0:T(8,128)(2,1)} %bitcast.289), channel_id=1, source_target_pairs={{0,2},{2,0},{1,3},{3,1},{4,6},{6,4},{5,7},{7,5},{8,10},{10,8},{9,1... | collective-permute-start | bytes 786440 | tf_op jit(solution)/shard_map/ppermute | solution.py:40
  177.6 100.5 %reduce-scatter.14.cloned.1.call-start = ((), (), s32[]{:S(2)}) async-start(), calls=%async_computation.9 | async-start | bytes 1310720 | tf_op jit(solution)/shard_map/reduce_scatter | solution.py:129
  204.9 7.9 %collective-permute-start.11 = (bf16[512,256]{0,1:T(8,128)(2,1)S(1)}, bf16[512,256]{0,1:T(8,128)(2,1)S(1)}, u32[]{:S(2)}, u32[]{:S(2)}) collective-permute-start(bf16[512,256]{0,1:T(8,128)(2,1)S(1)} %get-tuple-element.18), channel_id=1, source_target_pairs={{0,4},{4,0},{1,5},{5,1},{2,6},{6,2},{3,7},{7,3},{8,12},{12,8},{9,1... | collective-permute-start | bytes 786440 | tf_op jit(solution)/shard_map/ppermute | solution.py:40
  220.8 7.0 %collective-permute-start.16 = (bf16[2,512,128]{2,1,0:T(8,128)(2,1)S(1)}, bf16[2,512,128]{2,1,0:T(8,128)(2,1)S(1)}, u32[]{:S(2)}, u32[]{:S(2)}) collective-permute-start(bf16[2,512,128]{2,1,0:T(8,128)(2,1)S(1)} %maximum_select_fusion.13), channel_id=1, source_target_pairs={{0,2},{2,0},{1,3},{3,1},{4,6},{6,4},{5,7},{7,5},{8,10},{10,8},{9,1... | collective-permute-start | bytes 786440 | tf_op jit(solution)/shard_map/ppermute | solution.py:40
  278.1 11.2 %collective-permute-start.18 = (bf16[512,256]{0,1:T(8,128)(2,1)}, bf16[512,256]{0,1:T(8,128)(2,1)S(1)}, u32[]{:S(2)}, u32[]{:S(2)}) collective-permute-start(bf16[512,256]{0,1:T(8,128)(2,1)} %reduce-scatter.14.cloned.1.call-done), channel_id=1, source_target_pairs={{0,8},{8,16},{16,24},{24,0},{1,9},{9,17},{17,25},{25,1},{2,10},{10... | collective-permute-start | bytes 786440 | tf_op jit(solution)/shard_map/ppermute | solution.py:19
  278.1 13.5 %collective-permute-start.19 = (bf16[512,256]{0,1:T(8,128)(2,1)}, bf16[512,256]{0,1:T(8,128)(2,1)S(1)}, u32[]{:S(2)}, u32[]{:S(2)}) collective-permute-start(bf16[512,256]{0,1:T(8,128)(2,1)} %reduce-scatter.14.cloned.1.call-done), channel_id=1, source_target_pairs={{0,24},{8,0},{16,8},{24,16},{1,25},{9,1},{17,9},{25,17},{2,26},{10... | collective-permute-start | bytes 786440 | tf_op jit(solution)/shard_map/ppermute | solution.py:26
  289.3 9.7 %collective-permute-start.20 = (bf16[512,256]{0,1:T(8,128)(2,1)S(1)}, bf16[512,256]{0,1:T(8,128)(2,1)S(1)}, u32[]{:S(2)}, u32[]{:S(2)}) collective-permute-start(bf16[512,256]{0,1:T(8,128)(2,1)S(1)} %collective-permute-done.18), channel_id=1, source_target_pairs={{0,8},{8,16},{16,24},{24,0},{1,9},{9,17},{17,25},{25,1},{2,10},{10... | collective-permute-start | bytes 786440 | tf_op jit(solution)/shard_map/ppermute | solution.py:19
  325.8 10.4 %collective-permute-start.21 = (bf16[2,2,512,256]{2,3,0,1:T(8,128)(2,1)}, bf16[2,2,512,256]{2,3,0,1:T(8,128)(2,1)S(1)}, u32[]{:S(2)}, u32[]{:S(2)}) collective-permute-start(bf16[2,2,512,256]{2,3,0,1:T(8,128)(2,1)} %fusion.100), channel_id=1, source_target_pairs={{0,1},{1,0},{2,3},{3,2},{4,5},{5,4},{6,7},{7,6},{8,9},{9,8},{10,11... | collective-permute-start | bytes 3145736 | tf_op jit(solution)/shard_map/ppermute | solution.py:40
  336.8 8.8 %collective-permute-start.22 = (bf16[2,512,128]{1,2,0:T(8,128)(2,1)S(1)}, bf16[2,512,128]{1,2,0:T(8,128)(2,1)S(1)}, u32[]{:S(2)}, u32[]{:S(2)}) collective-permute-start(bf16[2,512,128]{1,2,0:T(8,128)(2,1)S(1)} %fusion.116), channel_id=1, source_target_pairs={{0,4},{4,0},{1,5},{5,1},{2,6},{6,2},{3,7},{7,3},{8,12},{12,8},{9,1... | collective-permute-start | bytes 786440 | tf_op jit(solution)/shard_map/ppermute | solution.py:40
  338.3 8.9 %collective-permute-start.24 = (bf16[2,512,128]{1,2,0:T(8,128)(2,1)S(1)}, bf16[2,512,128]{1,2,0:T(8,128)(2,1)S(1)}, u32[]{:S(2)}, u32[]{:S(2)}) collective-permute-start(bf16[2,512,128]{1,2,0:T(8,128)(2,1)S(1)} %fusion.117), channel_id=1, source_target_pairs={{0,2},{2,0},{1,3},{3,1},{4,6},{6,4},{5,7},{7,5},{8,10},{10,8},{9,1... | collective-permute-start | bytes 786440 | tf_op jit(solution)/shard_map/ppermute | solution.py:40
  361.3 11.0 %collective-permute-start.27 = (bf16[512,256]{0,1:T(8,128)(2,1)S(1)}, bf16[512,256]{0,1:T(8,128)(2,1)S(1)}, u32[]{:S(2)}, u32[]{:S(2)}) collective-permute-start(bf16[512,256]{0,1:T(8,128)(2,1)S(1)} %get-tuple-element.17), channel_id=1, source_target_pairs={{0,8},{8,16},{16,24},{24,0},{1,9},{9,17},{17,25},{25,1},{2,10},{10... | collective-permute-start | bytes 786440 | tf_op jit(solution)/shard_map/ppermute | solution.py:19
  361.4 13.0 %collective-permute-start.28 = (bf16[512,256]{0,1:T(8,128)(2,1)S(1)}, bf16[512,256]{0,1:T(8,128)(2,1)S(1)}, u32[]{:S(2)}, u32[]{:S(2)}) collective-permute-start(bf16[512,256]{0,1:T(8,128)(2,1)S(1)} %get-tuple-element.17), channel_id=1, source_target_pairs={{0,24},{8,0},{16,8},{24,16},{1,25},{9,1},{17,9},{25,17},{2,26},{10... | collective-permute-start | bytes 786440 | tf_op jit(solution)/shard_map/ppermute | solution.py:26
  372.4 8.4 %collective-permute-start.29 = (bf16[512,256]{0,1:T(8,128)(2,1)S(1)}, bf16[512,256]{0,1:T(8,128)(2,1)S(1)}, u32[]{:S(2)}, u32[]{:S(2)}) collective-permute-start(bf16[512,256]{0,1:T(8,128)(2,1)S(1)} %collective-permute-done.27), channel_id=1, source_target_pairs={{0,8},{8,16},{16,24},{24,0},{1,9},{9,17},{17,25},{25,1},{2,10},{10... | collective-permute-start | bytes 786440 | tf_op jit(solution)/shard_map/ppermute | solution.py:19
  396.4 8.3 %collective-permute-start.31 = (bf16[512,256]{0,1:T(8,128)(2,1)S(1)}, bf16[512,256]{0,1:T(8,128)(2,1)S(1)}, u32[]{:S(2)}, u32[]{:S(2)}) collective-permute-start(bf16[512,256]{0,1:T(8,128)(2,1)S(1)} %fusion.118), channel_id=1, source_target_pairs={{0,2},{2,0},{1,3},{3,1},{4,6},{6,4},{5,7},{7,5},{8,10},{10,8},{9,1... | collective-permute-start | bytes 786440 | tf_op jit(solution)/shard_map/ppermute | solution.py:40
  405.0 11.0 %collective-permute-start.32 = (bf16[512,256]{0,1:T(8,128)(2,1)S(1)}, bf16[512,256]{0,1:T(8,128)(2,1)S(1)}, u32[]{:S(2)}, u32[]{:S(2)}) collective-permute-start(bf16[512,256]{0,1:T(8,128)(2,1)S(1)} %get-tuple-element.15), channel_id=1, source_target_pairs={{0,8},{8,16},{16,24},{24,0},{1,9},{9,17},{17,25},{25,1},{2,10},{10... | collective-permute-start | bytes 786440 | tf_op jit(solution)/shard_map/ppermute | solution.py:19
  405.1 13.0 %collective-permute-start.33 = (bf16[512,256]{0,1:T(8,128)(2,1)S(1)}, bf16[512,256]{0,1:T(8,128)(2,1)S(1)}, u32[]{:S(2)}, u32[]{:S(2)}) collective-permute-start(bf16[512,256]{0,1:T(8,128)(2,1)S(1)} %get-tuple-element.15), channel_id=1, source_target_pairs={{0,24},{8,0},{16,8},{24,16},{1,25},{9,1},{17,9},{25,17},{2,26},{10... | collective-permute-start | bytes 786440 | tf_op jit(solution)/shard_map/ppermute | solution.py:26
  416.0 9.5 %collective-permute-start.34 = (bf16[512,256]{0,1:T(8,128)(2,1)S(1)}, bf16[512,256]{0,1:T(8,128)(2,1)S(1)}, u32[]{:S(2)}, u32[]{:S(2)}) collective-permute-start(bf16[512,256]{0,1:T(8,128)(2,1)S(1)} %collective-permute-done.32), channel_id=1, source_target_pairs={{0,8},{8,16},{16,24},{24,0},{1,9},{9,17},{17,25},{25,1},{2,10},{10... | collective-permute-start | bytes 786440 | tf_op jit(solution)/shard_map/ppermute | solution.py:19
  440.2 9.2 %collective-permute-start.36 = (bf16[512,256]{0,1:T(8,128)(2,1)S(1)}, bf16[512,256]{0,1:T(8,128)(2,1)S(1)}, u32[]{:S(2)}, u32[]{:S(2)}) collective-permute-start(bf16[512,256]{0,1:T(8,128)(2,1)S(1)} %fusion.119), channel_id=1, source_target_pairs={{0,2},{2,0},{1,3},{3,1},{4,6},{6,4},{5,7},{7,5},{8,10},{10,8},{9,1... | collective-permute-start | bytes 786440 | tf_op jit(solution)/shard_map/ppermute | solution.py:40
  441.4 13.6 %collective-permute-start.38 = (bf16[512,256]{0,1:T(8,128)(2,1)}, bf16[512,256]{0,1:T(8,128)(2,1)S(1)}, u32[]{:S(2)}, u32[]{:S(2)}) collective-permute-start(bf16[512,256]{0,1:T(8,128)(2,1)} %copy-done.10), channel_id=1, source_target_pairs={{0,2},{2,0},{1,3},{3,1},{4,6},{6,4},{5,7},{7,5},{8,10},{10,8},{9,1... | collective-permute-start | bytes 786440 | tf_op jit(solution)/shard_map/ppermute | solution.py:40
  449.5 10.2 %collective-permute-start.37 = (bf16[512,256]{0,1:T(8,128)(2,1)S(1)}, bf16[512,256]{0,1:T(8,128)(2,1)S(1)}, u32[]{:S(2)}, u32[]{:S(2)}) collective-permute-start(bf16[512,256]{0,1:T(8,128)(2,1)S(1)} %get-tuple-element.12), channel_id=1, source_target_pairs={{0,2},{2,0},{1,3},{3,1},{4,6},{6,4},{5,7},{7,5},{8,10},{10,8},{9,1... | collective-permute-start | bytes 786440 | tf_op jit(solution)/shard_map/ppermute | solution.py:40
  465.1 11.0 %collective-permute-start.39 = (bf16[512,256]{0,1:T(8,128)(2,1)S(1)}, bf16[512,256]{0,1:T(8,128)(2,1)S(1)}, u32[]{:S(2)}, u32[]{:S(2)}) collective-permute-start(bf16[512,256]{0,1:T(8,128)(2,1)S(1)} %get-tuple-element.11), channel_id=1, source_target_pairs={{0,8},{8,16},{16,24},{24,0},{1,9},{9,17},{17,25},{25,1},{2,10},{10... | collective-permute-start | bytes 786440 | tf_op jit(solution)/shard_map/ppermute | solution.py:19
  465.1 13.0 %collective-permute-start.40 = (bf16[512,256]{0,1:T(8,128)(2,1)S(1)}, bf16[512,256]{0,1:T(8,128)(2,1)S(1)}, u32[]{:S(2)}, u32[]{:S(2)}) collective-permute-start(bf16[512,256]{0,1:T(8,128)(2,1)S(1)} %get-tuple-element.11), channel_id=1, source_target_pairs={{0,24},{8,0},{16,8},{24,16},{1,25},{9,1},{17,9},{25,17},{2,26},{10... | collective-permute-start | bytes 786440 | tf_op jit(solution)/shard_map/ppermute | solution.py:26
  476.1 9.5 %collective-permute-start.41 = (bf16[512,256]{0,1:T(8,128)(2,1)S(1)}, bf16[512,256]{0,1:T(8,128)(2,1)S(1)}, u32[]{:S(2)}, u32[]{:S(2)}) collective-permute-start(bf16[512,256]{0,1:T(8,128)(2,1)S(1)} %collective-permute-done.39), channel_id=1, source_target_pairs={{0,8},{8,16},{16,24},{24,0},{1,9},{9,17},{17,25},{25,1},{2,10},{10... | collective-permute-start | bytes 786440 | tf_op jit(solution)/shard_map/ppermute | solution.py:19
  493.6 11.1 %collective-permute-start.43 = (bf16[512,256]{0,1:T(8,128)(2,1)S(1)}, bf16[512,256]{0,1:T(8,128)(2,1)S(1)}, u32[]{:S(2)}, u32[]{:S(2)}) collective-permute-start(bf16[512,256]{0,1:T(8,128)(2,1)S(1)} %get-tuple-element.9), channel_id=1, source_target_pairs={{0,8},{8,16},{16,24},{24,0},{1,9},{9,17},{17,25},{25,1},{2,10},{10... | collective-permute-start | bytes 786440 | tf_op jit(solution)/shard_map/ppermute | solution.py:19
  493.7 14.0 %collective-permute-start.44 = (bf16[512,256]{0,1:T(8,128)(2,1)S(1)}, bf16[512,256]{0,1:T(8,128)(2,1)S(1)}, u32[]{:S(2)}, u32[]{:S(2)}) collective-permute-start(bf16[512,256]{0,1:T(8,128)(2,1)S(1)} %get-tuple-element.9), channel_id=1, source_target_pairs={{0,24},{8,0},{16,8},{24,16},{1,25},{9,1},{17,9},{25,17},{2,26},{10... | collective-permute-start | bytes 786440 | tf_op jit(solution)/shard_map/ppermute | solution.py:26
  504.7 10.4 %collective-permute-start.45 = (bf16[512,256]{0,1:T(8,128)(2,1)S(1)}, bf16[512,256]{0,1:T(8,128)(2,1)S(1)}, u32[]{:S(2)}, u32[]{:S(2)}) collective-permute-start(bf16[512,256]{0,1:T(8,128)(2,1)S(1)} %collective-permute-done.43), channel_id=1, source_target_pairs={{0,8},{8,16},{16,24},{24,0},{1,9},{9,17},{17,25},{25,1},{2,10},{10... | collective-permute-start | bytes 786440 | tf_op jit(solution)/shard_map/ppermute | solution.py:19
  (41 other events, 238.8 us)
Sparse Core Ops, SparseCore 0:
  22.5 29.8 reduce-scatter.5
  63.8 25.7 reduce-scatter.7
  125.4 26.4 reduce-scatter.9
  177.7 26.1 reduce-scatter.11
  253.1 24.9 reduce-scatter.13
